TPU v7x, 32 devices: a whole 2x2x4 slice. The times are simulated.
32 devices in a mesh: shot: 2 (over core), gy: 4 (over y, x), gx: 4 (over z).
Axes of the slice: x: 2, y: 2, z: 4, core: 2. Of those that a mesh axis runs over, the one named last changes fastest.
Arguments:
- fwd_prev: float32 [2, 4, 1024, 512], P('shot', None, 'gy', 'gx'), may hold values from -6 to 6
- fwd_cur: float32 [2, 4, 1024, 512], P('shot', None, 'gy', 'gx'), may hold values from -6 to 6
- adj_late: float32 [2, 4, 1024, 512], P('shot', None, 'gy', 'gx'), may hold values from -6 to 6
- adj_now: float32 [2, 4, 1024, 512], P('shot', None, 'gy', 'gx'), may hold values from -6 to 6
- courant: float32 [4, 1024, 512], P(None, 'gy', 'gx'), may hold values from 0.02 to 0.19
- wavelet: float32 [2, 2], P('shot'), may hold values from -16 to 16
- boxes: int32 [2, 4], P('shot'), may hold values from 0 to 1024, as said below
- sources: int32 [2, 3], P('shot'), may hold values from 0 to 1023, as said below
- slab_top: int32 [1], replicated, may hold values from 0 to 508
Outputs:
- gradient: float32 [2, 512, 256], P(None, 'gy', 'gx')
Inputs may be any that keep to these rules, and one draw needn't show every extreme that they name: `boxes`: shot s's box is y0 <= y < y1, x0 <= x < x1 with y0 < y1 <= 1024, x0 < x1 <= 512, every bound a multiple of 16. `sources`: each shot's source cell (z, y, x) lies in the slab and inside that shot's box.
All inputs are finite; a program needn't handle non-finite values.
Results may differ from a plain program's by a relative error of at most 0.0003.
Values sent between devices are 32-bit elements; how exact they have to be, the bound alone decides.
A program may use at most 128 MiB of HBM per device.

v0:
```python
import jax
import jax.numpy as jnp
from jax import lax
from jax.sharding import PartitionSpec as P

COEFFS = (-205.0 / 72.0, 8.0 / 5.0, -1.0 / 5.0, 8.0 / 315.0, -1.0 / 560.0)


def with_halo(cells, sides, width):
    for axis, dim in sides:
        count = lax.axis_size(axis)
        ends = count - 1
        head = lax.slice_in_dim(cells, 0, width, axis=dim)
        tail = lax.slice_in_dim(cells, cells.shape[dim] - width, cells.shape[dim], axis=dim)
        cells = jnp.concatenate(
            [
                lax.ppermute(tail, axis, [(i, (i + 1) % count) for i in range(ends)]),
                cells,
                lax.ppermute(head, axis, [((i + 1) % count, i) for i in range(ends)]),
            ],
            axis=dim,
        )
    return cells


def stencil(padded):
    depth_count = padded.shape[1]
    out_y = padded.shape[2] - 8
    out_x = padded.shape[3] - 8
    deep_pad = jnp.pad(padded[:, :, 4 : 4 + out_y, 4 : 4 + out_x], ((0, 0), (4, 4), (0, 0), (0, 0)))
    summed = 3.0 * COEFFS[0] * deep_pad[:, 4 : 4 + depth_count]
    for offset in range(1, 5):
        neighbours = (
            deep_pad[:, 4 + offset : 4 + offset + depth_count]
            + deep_pad[:, 4 - offset : 4 - offset + depth_count]
        )
        neighbours = neighbours + padded[:, :, 4 + offset : 4 + offset + out_y, 4 : 4 + out_x]
        neighbours = neighbours + padded[:, :, 4 - offset : 4 - offset + out_y, 4 : 4 + out_x]
        neighbours = neighbours + padded[:, :, 4 : 4 + out_y, 4 + offset : 4 + offset + out_x]
        neighbours = neighbours + padded[:, :, 4 : 4 + out_y, 4 - offset : 4 - offset + out_x]
        summed = summed + COEFFS[offset] * neighbours
    return summed


def per_device(fwd_prev, fwd_cur, adj_late, adj_now, courant, wavelet, boxes, sources, slab_top):
    shot_count, depth_count, span_y, span_x = fwd_cur.shape
    anchor_y = lax.axis_index("gy") * span_y
    anchor_x = lax.axis_index("gx") * span_x
    boxes_twice = jnp.concatenate([boxes, boxes], 0)

    def box_mask(margin, box_rows):
        cells_y = anchor_y - margin + jnp.arange(span_y + 2 * margin, dtype=jnp.int32)
        cells_x = anchor_x - margin + jnp.arange(span_x + 2 * margin, dtype=jnp.int32)
        inside_y = (
            (cells_y[None, :] >= box_rows[:, 0:1]) & (cells_y[None, :] < box_rows[:, 1:2])
        ).astype(jnp.float32)
        inside_x = (
            (cells_x[None, :] >= box_rows[:, 2:3]) & (cells_x[None, :] < box_rows[:, 3:4])
        ).astype(jnp.float32)
        return inside_y[:, None, :, None] * inside_x[:, None, None, :]

    def source_term(margin, column):
        cells_y = anchor_y - margin + jnp.arange(span_y + 2 * margin, dtype=jnp.int32)
        cells_x = anchor_x - margin + jnp.arange(span_x + 2 * margin, dtype=jnp.int32)
        cells_z = jnp.arange(depth_count, dtype=jnp.int32)
        onehot_z = (cells_z[None, :] == sources[:, 0:1]).astype(jnp.float32)
        onehot_y = (cells_y[None, :] == sources[:, 1:2]).astype(jnp.float32)
        onehot_x = (cells_x[None, :] == sources[:, 2:3]).astype(jnp.float32)
        weighted = onehot_z * wavelet[:, column : column + 1]
        source_field = (
            weighted[:, :, None, None] * onehot_y[:, None, :, None] * onehot_x[:, None, None, :]
        )
        source_field = jnp.concatenate([source_field, jnp.zeros_like(source_field)], 0)
        return source_field

    stacked_before = jnp.concatenate([fwd_prev, adj_late, courant[None]], 0)
    current = jnp.concatenate([fwd_cur, adj_now], 0)
    older_wide = with_halo(stacked_before, (("gy", 2), ("gx", 3)), 4)
    newer_wide = with_halo(current, (("gy", 2), ("gx", 3)), 8)
    speed_wide = older_wide[2 * shot_count :]
    update = (
        2.0 * newer_wide[:, :, 4:-4, 4:-4]
        - older_wide[: 2 * shot_count]
        + speed_wide * stencil(newer_wide)
    )
    update = update + source_term(4, 0)
    middle = box_mask(4, boxes_twice) * update
    interior = middle[:, :, 4:-4, 4:-4]
    update = 2.0 * interior - current + courant * stencil(middle)
    update = update + source_term(0, 1)
    latest = box_mask(0, boxes_twice) * update
    fwd_mid, adj_mid = (interior[:shot_count], interior[shot_count:])
    fwd_last, adj_first = (latest[:shot_count], latest[shot_count:])
    image_cell = adj_first * (fwd_mid - 2.0 * fwd_cur + fwd_prev) + adj_mid * (
        fwd_last - 2.0 * fwd_mid + fwd_cur
    )
    coarse = image_cell.reshape(
        shot_count, depth_count // 2, 2, span_y // 2, 2, span_x // 2, 2
    ).mean(axis=(2, 4, 6))
    coarse = jnp.sum(coarse, axis=0)
    depth_index = (
        slab_top[0].astype(jnp.float32)
        + 2.0 * jnp.arange(depth_count // 2).astype(jnp.float32)
        + 1.0
    )
    factor = (0.25 + depth_index / 128.0)[:, None, None]
    total = lax.psum(coarse, "shot")
    return total * factor


def solution(mesh):
    return jax.shard_map(
        per_device,
        mesh=mesh,
        in_specs=(
            P("shot", None, "gy", "gx"),
            P("shot", None, "gy", "gx"),
            P("shot", None, "gy", "gx"),
            P("shot", None, "gy", "gx"),
            P(None, "gy", "gx"),
            P("shot", None),
            P("shot", None),
            P("shot", None),
            P(),
        ),
        out_specs=P(None, "gy", "gx"),
        check_vma=False,
    )
```

profile of v0, /device:TPU:0, one launch (start us, length us, event | category | flops | bytes accessed | tf_op | source)
XLA Modules:
  0.0 153.4 jit_solution(927272376209038710)
XLA Ops:
  6.5 1.3 copy.38
  7.8 1.2 copy.39
  10.0 5.0 %collective-permute-start.4 = (f32[3,4,4,128]{3,2,1,0:T(4,128)S(1)}, f32[3,4,4,128]{3,2,1,0:T(4,128)S(1)}, u32[]{:S(2)}, u32[]{:S(2)}) collective-permute-start(f32[3,4,4,128]{3,2,1,0:T(4,128)S(1)} %copy.41), channel_id=1, source_target_pairs={{0,4},{4,8},{8,12},{1,5},{5,9},{9,13},{2,6},{6,10},{10,14},{3,7},{... | collective-permute-start | bytes 73736 | tf_op jit(solution)/shard_map/ppermute | solution.py:17
  15.3 1.3 collective-permute-start.5
  16.6 1.2 copy.36
  18.1 1.1 fusion.57
  19.2 5.3 %collective-permute-start = (f32[2,4,8,128]{2,3,1,0:T(8,128)}, f32[2,4,8,128]{2,3,1,0:T(8,128)}, u32[]{:S(2)}, u32[]{:S(2)}) collective-permute-start(f32[2,4,8,128]{2,3,1,0:T(8,128)} %get-tuple-element.15), channel_id=1, source_target_pairs={{0,4},{4,8},{8,12},{1,5},{5,9},{9,13},{2,6},{6,10},{10,14},{3,7},{... | collective-permute-start | bytes 98312 | tf_op jit(solution)/shard_map/ppermute | solution.py:17
  24.5 1.3 collective-permute-start.1
  30.1 0.9 broadcast_multiply_fusion.2
  30.9 1.8 %compare_select_fusion = (f32[4]{0:T(128)S(1)}, f32[4]{0:T(128)S(1)}) fusion(f32[]{:T(128)} %bitcast.6, s32[]{:T(128)} %bitcast.2, f32[]{:T(128)} %bitcast.3), kind=kLoop, calls=%fused_computation.124 | loop fusion | flops 12 | bytes 44 | tf_op jit(solution)/shard_map/mul | solution.py:69
  32.8 1.0 broadcast_multiply_fusion
  33.9 0.9 broadcast_multiply_fusion.1
  34.9 0.8 broadcast_multiply_fusion.3
  36.6 1.2 copy.44
  37.8 1.0 pad_maximum_fusion.20
  38.8 3.6 %collective-permute-start.6 = (f32[3,4,264,4]{2,3,1,0:T(4,128)S(1)}, f32[3,4,264,4]{2,3,1,0:T(4,128)S(1)}, u32[]{:S(2)}, u32[]{:S(2)}) collective-permute-start(f32[3,4,264,4]{2,3,1,0:T(4,128)S(1)} %get-tuple-element.9), channel_id=1, source_target_pairs={{0,1},{1,2},{2,3},{4,5},{5,6},{6,7},{8,9},{9,10},{10,11},{12,13},{... | collective-permute-start | bytes 152072 | tf_op jit(solution)/shard_map/ppermute | solution.py:17
  42.5 1.3 collective-permute-start.7
  43.8 5.0 %collective-permute-done.1 = f32[2,4,8,128]{2,3,1,0:T(8,128)} collective-permute-done((f32[2,4,8,128]{2,3,1,0:T(8,128)}, f32[2,4,8,128]{2,3,1,0:T(8,128)}, u32[]{:S(2)}, u32[]{:S(2)}) %collective-permute-start.1) | collective-permute-done | bytes 32800 | tf_op jit(solution)/shard_map/ppermute | solution.py:19
  48.7 0.9 pad_maximum_fusion.12
  49.7 3.5 %collective-permute-start.2 = (f32[2,4,272,8]{2,3,1,0:T(8,128)S(1)}, f32[2,4,272,8]{2,3,1,0:T(8,128)S(1)}, u32[]{:S(2)}, u32[]{:S(2)}) collective-permute-start(f32[2,4,272,8]{2,3,1,0:T(8,128)S(1)} %get-tuple-element.12), channel_id=1, source_target_pairs={{0,1},{1,2},{2,3},{4,5},{5,6},{6,7},{8,9},{9,10},{10,11},{12,13},{... | collective-permute-start | bytes 208904 | tf_op jit(solution)/shard_map/ppermute | solution.py:17
  53.2 1.5 collective-permute-start.3
  54.7 2.5 %pad_maximum_fusion = f32[3,4,264,136]{2,3,1,0:T(8,128)} fusion(f32[3,4,264,4]{2,3,1,0:T(4,128)S(1)} %collective-permute-done.7, f32[3,4,4,128]{2,3,1,0:T(8,128)S(1)} %copy-done, f32[1,4,256,128]{2,3,1,0:T(8,128)S(1)} %bitcast.13, f32[1,4,256,128]{2,3,1,0:T(8,128)S(1)} %copy.40, f32[1,4,256,128]{2,3,1,0:T(8,128)S(1)} %copy.39, ...), kind=kLoop, calls=%fused_computation.12 | loop fusion | flops 2585088 | bytes 3446784 | tf_op jit(solution)/shard_map/concatenate | solution.py:15
  57.2 1.3 maximum_bitcast_fusion
  58.4 1.2 collective-permute-done.3
  60.3 1.8 %pad_maximum_fusion.1 = f32[2,4,272,144]{2,3,1,0:T(8,128)S(1)} fusion(f32[2,4,272,8]{2,3,1,0:T(8,128)S(1)} %collective-permute-done.3, f32[2,4,8,128]{2,3,1,0:T(8,128)} %collective-permute-done.1, f32[1,4,256,128]{2,3,1,0:T(8,128)S(1)} %copy.37, f32[1,4,256,128]{2,3,1,0:T(8,128)S(1)} %copy.36, f32[2,4,8,128]{2,3,1,0:T(8,128)} %collective-permute-done, ...), kind=kLoop, calls=%fused_computation.13 | loop fusion | flops 1566720 | bytes 2506752 | tf_op jit(solution)/shard_map/concatenate | solution.py:15
  63.2 10.9 %fusion.28 = f32[2,4,264,136]{2,3,1,0:T(8,128)S(1)} fusion(f32[1,4,264,136]{2,3,1,0:T(8,128)} %broadcast_multiply_fusion, f32[2,4,8,128]{2,3,1,0:T(8,128)} %collective-permute-done.1, f32[1,4,256,128]{2,3,1,0:T(8,128)S(1)} %copy.37, f32[1,4,256,128]{2,3,1,0:T(8,128)S(1)} %copy.36, f32[2,4,8,128]{2,3,1,0:T(8,128)} %collective-permute-done, ...), kind=kLoop, calls=%fused_computation.52 | loop fusion | flops 11776512 | bytes 22221312 | tf_op jit(solution)/shard_map/mul | solution.py:87
  74.4 0.7 copy-done.1
  75.2 4.3 %fusion.32 = f32[2,4,256,128]{2,3,1,0:T(8,128)S(1)} fusion(f32[1,4,256,128]{2,3,1,0:T(8,128)S(1)} %copy.37, f32[1,4,256,128]{2,3,1,0:T(8,128)S(1)} %copy.36, f32[2,4,256,128]{2,3,1,0:T(8,128)S(1)} %slice.317, f32[2,4,264,136]{2,3,1,0:T(8,128)S(1)} %fusion.28, f32[1,4,256,128]{2,3,1,0:T(8,128)S(1)} %copy-done.1, f32[4,256,128]{1,2,0:T(8,128)S(1)} %copy.38, ...), kind=kLoop, calls=%fused_computation.62 | loop fusion | flops 8912896 | bytes 21233664 | tf_op jit(solution)/shard_map/mul | solution.py:91
  80.1 34.8 %reshape.410 = f32[2,2,128,2,64,2]{5,4,3,2,1,0:T(8,128)} reshape(f32[1,4,256,128]{3,2,1,0:T(8,128)S(1)} %copy.49) | data formatting | bytes 1048576 | tf_op jit(solution)/shard_map/reshape | solution.py:97
  114.9 12.2 %reduce_sum.8 = f32[2,128,64]{2,1,0:T(8,128)S(1)} reduce(f32[2,2,128,2,64,2]{5,4,3,2,1,0:T(8,128)} %reshape.410, f32[]{:T(128)} %constant.23.clone.1), dimensions={1,3,5}, to_apply=%region_0.1 | reduce | flops 114688 | bytes 589828 | tf_op jit(solution)/shard_map/reduce_sum | solution.py:99
  127.9 17.1 %all-reduce.6.cloned.1.call-done = f32[2,128,64]{1,2,0:T(8,128)} async-done(((f32[2,128,64]{1,2,0:T(8,128)}), f32[2,128,64]{1,2,0:T(8,128)}) %all-reduce.6.cloned.1.call-update) | async-done | bytes 65552 | tf_op jit(solution)/shard_map/psum | solution.py:107
  145.0 1.5 %broadcast_multiply_fusion.4 = f32[2,128,64]{1,2,0:T(8,128)} fusion(f32[2,128,64]{1,2,0:T(8,128)} %all-reduce.6.cloned.1.call-done, f32[2]{0:T(128)S(1)} %multiply_add_fusion), kind=kLoop, calls=%fused_computation.111 | loop fusion | flops 16384 | bytes 131080 | tf_op jit(solution)/shard_map/mul | solution.py:108
  (61 shorter events, 9.4 us)
Async XLA Ops:
  6.5 2.6 %copy-start.4 = (f32[1,4,256,128]{3,2,1,0:T(8,128)S(1)}, f32[1,4,256,128]{3,2,1,0:T(8,128)}, u32[]{:S(2)}) copy-start(f32[1,4,256,128]{3,2,1,0:T(8,128)} %param.11) | copy-start | bytes 1572868
  6.5 138.5 %all-reduce.6.cloned.1.call-start = ((), (), s32[]{:S(2)}) async-start(), calls=%async_computation | async-start | bytes 131072 | tf_op jit(solution)/shard_map/psum | solution.py:107
  10.0 7.8 %copy-start.5 = (f32[1,4,256,128]{3,2,1,0:T(8,128)S(1)}, f32[1,4,256,128]{3,2,1,0:T(8,128)}, u32[]{:S(2)}) copy-start(f32[1,4,256,128]{3,2,1,0:T(8,128)} %param.12) | copy-start | bytes 1572868
  10.0 26.3 %collective-permute-start.4 = (f32[3,4,4,128]{3,2,1,0:T(4,128)S(1)}, f32[3,4,4,128]{3,2,1,0:T(4,128)S(1)}, u32[]{:S(2)}, u32[]{:S(2)}) collective-permute-start(f32[3,4,4,128]{3,2,1,0:T(4,128)S(1)} %copy.41), channel_id=1, source_target_pairs={{0,4},{4,8},{8,12},{1,5},{5,9},{9,13},{2,6},{6,10},{10,14},{3,7},{... | collective-permute-start | bytes 73736 | tf_op jit(solution)/shard_map/ppermute | solution.py:17
  15.3 21.3 %collective-permute-start.5 = (f32[3,4,4,128]{3,2,1,0:T(4,128)S(1)}, f32[3,4,4,128]{3,2,1,0:T(4,128)S(1)}, u32[]{:S(2)}, u32[]{:S(2)}) collective-permute-start(f32[3,4,4,128]{3,2,1,0:T(4,128)S(1)} %copy.42), channel_id=1, source_target_pairs={{4,0},{8,4},{12,8},{5,1},{9,5},{13,9},{6,2},{10,6},{14,10},{7,3},{... | collective-permute-start | bytes 73736 | tf_op jit(solution)/shard_map/ppermute | solution.py:19
  17.8 8.0 %copy-start.8 = (s32[1,3]{1,0:T(1,128)S(1)}, s32[1,3]{1,0:T(1,128)}, u32[]{:S(2)}) copy-start(s32[1,3]{1,0:T(1,128)} %param.16) | copy-start | bytes 40
  17.9 11.1 %copy-start.10 = (s32[1,4]{1,0:T(1,128)S(1)}, s32[1,4]{1,0:T(1,128)}, u32[]{:S(2)}) copy-start(s32[1,4]{1,0:T(1,128)} %param.15) | copy-start | bytes 52
  17.9 11.3 %copy-start.9 = (f32[1,2]{1,0:T(1,128)S(1)}, f32[1,2]{1,0:T(1,128)}, u32[]{:S(2)}) copy-start(f32[1,2]{1,0:T(1,128)} %param.14) | copy-start | bytes 28
  19.2 24.6 %collective-permute-start = (f32[2,4,8,128]{2,3,1,0:T(8,128)}, f32[2,4,8,128]{2,3,1,0:T(8,128)}, u32[]{:S(2)}, u32[]{:S(2)}) collective-permute-start(f32[2,4,8,128]{2,3,1,0:T(8,128)} %get-tuple-element.15), channel_id=1, source_target_pairs={{0,4},{4,8},{8,12},{1,5},{5,9},{9,13},{2,6},{6,10},{10,14},{3,7},{... | collective-permute-start | bytes 98312 | tf_op jit(solution)/shard_map/ppermute | solution.py:17
  24.5 24.2 %collective-permute-start.1 = (f32[2,4,8,128]{2,3,1,0:T(8,128)}, f32[2,4,8,128]{2,3,1,0:T(8,128)}, u32[]{:S(2)}, u32[]{:S(2)}) collective-permute-start(f32[2,4,8,128]{2,3,1,0:T(8,128)} %get-tuple-element.16), channel_id=1, source_target_pairs={{4,0},{8,4},{12,8},{5,1},{9,5},{13,9},{6,2},{10,6},{14,10},{7,3},{... | collective-permute-start | bytes 98312 | tf_op jit(solution)/shard_map/ppermute | solution.py:19
  38.8 15.9 %copy-start = (f32[3,4,4,128]{2,3,1,0:T(8,128)S(1)}, f32[3,4,4,128]{2,3,1,0:T(8,128)}, u32[]{:S(2)}) copy-start(f32[3,4,4,128]{2,3,1,0:T(8,128)} %copy.44) | copy-start | bytes 73732
  38.8 15.8 %collective-permute-start.6 = (f32[3,4,264,4]{2,3,1,0:T(4,128)S(1)}, f32[3,4,264,4]{2,3,1,0:T(4,128)S(1)}, u32[]{:S(2)}, u32[]{:S(2)}) collective-permute-start(f32[3,4,264,4]{2,3,1,0:T(4,128)S(1)} %get-tuple-element.9), channel_id=1, source_target_pairs={{0,1},{1,2},{2,3},{4,5},{5,6},{6,7},{8,9},{9,10},{10,11},{12,13},{... | collective-permute-start | bytes 152072 | tf_op jit(solution)/shard_map/ppermute | solution.py:17
  42.5 12.2 %collective-permute-start.7 = (f32[3,4,264,4]{2,3,1,0:T(4,128)S(1)}, f32[3,4,264,4]{2,3,1,0:T(4,128)S(1)}, u32[]{:S(2)}, u32[]{:S(2)}) collective-permute-start(f32[3,4,264,4]{2,3,1,0:T(4,128)S(1)} %get-tuple-element.10), channel_id=1, source_target_pairs={{1,0},{2,1},{3,2},{5,4},{6,5},{7,6},{9,8},{10,9},{11,10},{13,12},{... | collective-permute-start | bytes 152072 | tf_op jit(solution)/shard_map/ppermute | solution.py:19
  49.7 8.8 %collective-permute-start.2 = (f32[2,4,272,8]{2,3,1,0:T(8,128)S(1)}, f32[2,4,272,8]{2,3,1,0:T(8,128)S(1)}, u32[]{:S(2)}, u32[]{:S(2)}) collective-permute-start(f32[2,4,272,8]{2,3,1,0:T(8,128)S(1)} %get-tuple-element.12), channel_id=1, source_target_pairs={{0,1},{1,2},{2,3},{4,5},{5,6},{6,7},{8,9},{9,10},{10,11},{12,13},{... | collective-permute-start | bytes 208904 | tf_op jit(solution)/shard_map/ppermute | solution.py:17
  53.2 6.5 %collective-permute-start.3 = (f32[2,4,272,8]{2,3,1,0:T(8,128)S(1)}, f32[2,4,272,8]{2,3,1,0:T(8,128)S(1)}, u32[]{:S(2)}, u32[]{:S(2)}) collective-permute-start(f32[2,4,272,8]{2,3,1,0:T(8,128)S(1)} %get-tuple-element.11), channel_id=1, source_target_pairs={{1,0},{2,1},{3,2},{5,4},{6,5},{7,6},{9,8},{10,9},{11,10},{13,12},{... | collective-permute-start | bytes 208904 | tf_op jit(solution)/shard_map/ppermute | solution.py:19
  59.7 0.6 copy-start.6
  62.1 1.0 copy-start.2
  62.2 1.0 copy-start.7
  74.1 1.0 copy-start.1
  74.1 1.1 copy-start.3
Sparse Core Ops, SparseCore 0:
  128.1 16.9 all-reduce.5
where the time goes:
time: 154 us; the launch traced here: 153 us
  other arithmetic  47.1 us (31%)
  local copies, waits for them, and re-layouts  45.7 us (30%)
  waiting for transfers between devices  23.3 us (15%)
  starting transfers between devices  22.8 us (15%)
  between operations  14.5 us (9%)
    reshape x1, local copies, waits for them, and re-layouts, per_device(): image_cell.reshape(shot_count, depth_count // 2, 2, span_y // 2, 2, span_...  34.8 us
    ppermute x4, starting transfers between devices, with_halo(): lax.ppermute(tail, axis, [(i, (i + 1) % count) for i in range(ends)])  17.4 us
    psum x1, waiting for transfers between devices, per_device(): total = lax.psum(coarse, 'shot')  17.1 us
    reduce_sum x1, other arithmetic, per_device(): coarse = image_cell.reshape(shot_count, depth_count // 2, 2, span_y // 2,...  12.2 us
    mul x1, other arithmetic, per_device(): middle = box_mask(4, boxes_twice) * update  10.9 us
    ppermute x4, waiting for transfers between devices, with_halo(): lax.ppermute(head, axis, [((i + 1) % count, i) for i in range(ends)])  6.23 us
    unnamed x27, local copies, waits for them, and re-layouts  5.99 us
    ppermute x4, starting transfers between devices, with_halo(): lax.ppermute(head, axis, [((i + 1) % count, i) for i in range(ends)])  5.34 us
  transfers between devices with their start and end apart: 9, of which 3 were waited for; matrix products, arithmetic and copies ran while one was open for 13% of the time, Pallas kernels for 0%

commit v1 on v0

--- a/solution.py
+++ b/solution.py
@@ -104,7 +104,8 @@
         + 1.0
     )
     factor = (0.25 + depth_index / 128.0)[:, None, None]
-    total = lax.psum(coarse, "shot")
+    parts = lax.all_gather(coarse, "shot", axis=0, tiled=False)
+    total = parts.sum(axis=0)
     return total * factor
 
 

time: 154 us -> 124 us (0.81)
  waiting for transfers between devices: 23.3 us -> 5.86 us
  between operations: 14.5 us -> 1.09 us
  blocking collectives: 0 us -> 1.9 us
    psum x1 -> x0, waiting for transfers between devices: 17.1 us -> none  [per_device(): total = lax.psum(coarse, 'shot')]
    all_gather x0 -> x1, blocking collectives: none -> 1.9 us  [per_device(): parts = lax.all_gather(coarse, 'shot', axis=0, tiled=False)]
  transfers between devices with their start and end apart: 9 -> 8, of which waited for: 3 -> 2; matrix products, arithmetic and copies ran while one was open for 13% -> 16% of each run, Pallas kernels for 0% -> 0%
where the time goes in v1:
time: 124 us; the launch traced here: 123 us
  other arithmetic  46 us (37%)
  local copies, waits for them, and re-layouts  45.8 us (37%)
  starting transfers between devices  22.8 us (18%)
  waiting for transfers between devices  5.86 us (5%)
  blocking collectives  1.9 us (2%)
    reshape x1, local copies, waits for them, and re-layouts, per_device(): image_cell.reshape(shot_count, depth_count // 2, 2, span_y // 2, 2, span_...  34.8 us
    ppermute x4, starting transfers between devices, with_halo(): lax.ppermute(tail, axis, [(i, (i + 1) % count) for i in range(ends)])  17.4 us
    reduce_sum x1, other arithmetic, per_device(): coarse = image_cell.reshape(shot_count, depth_count // 2, 2, span_y // 2,...  12.2 us
    mul x1, other arithmetic, per_device(): middle = box_mask(4, boxes_twice) * update  10.9 us
    unnamed x27, local copies, waits for them, and re-layouts  5.99 us
    ppermute x4, waiting for transfers between devices, with_halo(): lax.ppermute(head, axis, [((i + 1) % count, i) for i in range(ends)])  5.85 us
    ppermute x4, starting transfers between devices, with_halo(): lax.ppermute(head, axis, [((i + 1) % count, i) for i in range(ends)])  5.34 us
    concatenate x3, other arithmetic, with_halo(): jnp.concatenate([lax.ppermute(tail, axis, [(i, (i + 1) % count) for i in...  5.2 us
  transfers between devices with their start and end apart: 8, of which 2 were waited for; matrix products, arithmetic and copies ran while one was open for 16% of the time, Pallas kernels for 0%

profile of v1, /device:TPU:0, one launch (start us, length us, event | category | flops | bytes accessed | tf_op | source)
XLA Modules:
  0.0 123.4 jit_solution(15373923425586023670)
XLA Ops:
  0.0 1.3 %copy.37 = f32[4,256,128]{1,2,0:T(8,128)S(1)} copy(f32[4,256,128]{2,1,0:T(8,128)} %param.13) | data formatting | bytes 1048576 | tf_op args[4]
  1.3 1.2 %copy.38 = f32[1,4,256,128]{2,3,1,0:T(8,128)S(1)} copy(f32[1,4,256,128]{3,2,1,0:T(8,128)} %param.9) | data formatting | bytes 1048576 | tf_op args[0]
  3.5 5.0 %collective-permute-start.4 = (f32[3,4,4,128]{3,2,1,0:T(4,128)S(1)}, f32[3,4,4,128]{3,2,1,0:T(4,128)S(1)}, u32[]{:S(2)}, u32[]{:S(2)}) collective-permute-start(f32[3,4,4,128]{3,2,1,0:T(4,128)S(1)} %copy.40), channel_id=1, source_target_pairs={{0,4},{4,8},{8,12},{1,5},{5,9},{9,13},{2,6},{6,10},{10,14},{3,7},{... | collective-permute-start | bytes 73736 | tf_op jit(solution)/shard_map/ppermute | solution.py:17
  8.8 1.3 %collective-permute-start.5 = (f32[3,4,4,128]{3,2,1,0:T(4,128)S(1)}, f32[3,4,4,128]{3,2,1,0:T(4,128)S(1)}, u32[]{:S(2)}, u32[]{:S(2)}) collective-permute-start(f32[3,4,4,128]{3,2,1,0:T(4,128)S(1)} %copy.41), channel_id=1, source_target_pairs={{4,0},{8,4},{12,8},{5,1},{9,5},{13,9},{6,2},{10,6},{14,10},{7,3},{... | collective-permute-start | bytes 73736 | tf_op jit(solution)/shard_map/ppermute | solution.py:19
  10.1 1.2 %copy.35 = f32[1,4,256,128]{2,3,1,0:T(8,128)S(1)} copy(f32[1,4,256,128]{3,2,1,0:T(8,128)} %param.10) | data formatting | bytes 1048576 | tf_op args[1]
  11.5 1.1 fusion.57
  12.7 5.3 %collective-permute-start = (f32[2,4,8,128]{2,3,1,0:T(8,128)}, f32[2,4,8,128]{2,3,1,0:T(8,128)}, u32[]{:S(2)}, u32[]{:S(2)}) collective-permute-start(f32[2,4,8,128]{2,3,1,0:T(8,128)} %get-tuple-element.15), channel_id=1, source_target_pairs={{0,4},{4,8},{8,12},{1,5},{5,9},{9,13},{2,6},{6,10},{10,14},{3,7},{... | collective-permute-start | bytes 98312 | tf_op jit(solution)/shard_map/ppermute | solution.py:17
  18.0 1.3 %collective-permute-start.1 = (f32[2,4,8,128]{2,3,1,0:T(8,128)}, f32[2,4,8,128]{2,3,1,0:T(8,128)}, u32[]{:S(2)}, u32[]{:S(2)}) collective-permute-start(f32[2,4,8,128]{2,3,1,0:T(8,128)} %get-tuple-element.16), channel_id=1, source_target_pairs={{4,0},{8,4},{12,8},{5,1},{9,5},{13,9},{6,2},{10,6},{14,10},{7,3},{... | collective-permute-start | bytes 98312 | tf_op jit(solution)/shard_map/ppermute | solution.py:19
  21.3 0.7 compare_convert_fusion.2
  24.5 0.9 broadcast_multiply_fusion.2
  25.4 1.9 %compare_select_fusion = (f32[4]{0:T(128)S(1)}, f32[4]{0:T(128)S(1)}) fusion(f32[]{:T(128)} %bitcast.6, s32[]{:T(128)} %bitcast.2, f32[]{:T(128)} %bitcast.3), kind=kLoop, calls=%fused_computation.124 | loop fusion | flops 12 | bytes 44 | tf_op jit(solution)/shard_map/mul | solution.py:69
  27.3 1.0 broadcast_multiply_fusion
  28.4 0.8 broadcast_multiply_fusion.3
  29.3 0.9 broadcast_multiply_fusion.1
  30.5 1.2 copy.43
  31.7 1.0 pad_maximum_fusion.20
  32.7 3.6 %collective-permute-start.6 = (f32[3,4,264,4]{2,3,1,0:T(4,128)S(1)}, f32[3,4,264,4]{2,3,1,0:T(4,128)S(1)}, u32[]{:S(2)}, u32[]{:S(2)}) collective-permute-start(f32[3,4,264,4]{2,3,1,0:T(4,128)S(1)} %get-tuple-element.9), channel_id=1, source_target_pairs={{0,1},{1,2},{2,3},{4,5},{5,6},{6,7},{8,9},{9,10},{10,11},{12,13},{... | collective-permute-start | bytes 152072 | tf_op jit(solution)/shard_map/ppermute | solution.py:17
  36.3 1.3 %collective-permute-start.7 = (f32[3,4,264,4]{2,3,1,0:T(4,128)S(1)}, f32[3,4,264,4]{2,3,1,0:T(4,128)S(1)}, u32[]{:S(2)}, u32[]{:S(2)}) collective-permute-start(f32[3,4,264,4]{2,3,1,0:T(4,128)S(1)} %get-tuple-element.10), channel_id=1, source_target_pairs={{1,0},{2,1},{3,2},{5,4},{6,5},{7,6},{9,8},{10,9},{11,10},{13,12},{... | collective-permute-start | bytes 152072 | tf_op jit(solution)/shard_map/ppermute | solution.py:19
  37.6 4.6 %collective-permute-done.1 = f32[2,4,8,128]{2,3,1,0:T(8,128)} collective-permute-done((f32[2,4,8,128]{2,3,1,0:T(8,128)}, f32[2,4,8,128]{2,3,1,0:T(8,128)}, u32[]{:S(2)}, u32[]{:S(2)}) %collective-permute-start.1) | collective-permute-done | bytes 32800 | tf_op jit(solution)/shard_map/ppermute | solution.py:19
  42.2 0.9 pad_maximum_fusion.12
  43.2 3.5 %collective-permute-start.2 = (f32[2,4,272,8]{2,3,1,0:T(8,128)S(1)}, f32[2,4,272,8]{2,3,1,0:T(8,128)S(1)}, u32[]{:S(2)}, u32[]{:S(2)}) collective-permute-start(f32[2,4,272,8]{2,3,1,0:T(8,128)S(1)} %get-tuple-element.12), channel_id=1, source_target_pairs={{0,1},{1,2},{2,3},{4,5},{5,6},{6,7},{8,9},{9,10},{10,11},{12,13},{... | collective-permute-start | bytes 208904 | tf_op jit(solution)/shard_map/ppermute | solution.py:17
  46.7 1.5 %collective-permute-start.3 = (f32[2,4,272,8]{2,3,1,0:T(8,128)S(1)}, f32[2,4,272,8]{2,3,1,0:T(8,128)S(1)}, u32[]{:S(2)}, u32[]{:S(2)}) collective-permute-start(f32[2,4,272,8]{2,3,1,0:T(8,128)S(1)} %get-tuple-element.11), channel_id=1, source_target_pairs={{1,0},{2,1},{3,2},{5,4},{6,5},{7,6},{9,8},{10,9},{11,10},{13,12},{... | collective-permute-start | bytes 208904 | tf_op jit(solution)/shard_map/ppermute | solution.py:19
  48.2 2.5 %pad_maximum_fusion = f32[3,4,264,136]{2,3,1,0:T(8,128)} fusion(f32[3,4,264,4]{2,3,1,0:T(4,128)S(1)} %collective-permute-done.7, f32[3,4,4,128]{2,3,1,0:T(8,128)S(1)} %copy-done, f32[1,4,256,128]{2,3,1,0:T(8,128)S(1)} %bitcast.14, f32[1,4,256,128]{2,3,1,0:T(8,128)S(1)} %copy.39, f32[1,4,256,128]{2,3,1,0:T(8,128)S(1)} %copy.38, ...), kind=kLoop, calls=%fused_computation.12 | loop fusion | flops 2585088 | bytes 3446784 | tf_op jit(solution)/shard_map/concatenate | solution.py:15
  50.6 1.3 %maximum_bitcast_fusion = f32[4,264,136]{1,2,0:T(8,128)} fusion(f32[3,4,264,4]{2,3,1,0:T(4,128)S(1)} %collective-permute-done.7, f32[3,4,264,4]{2,3,1,0:T(4,128)S(1)} %collective-permute-done.6, f32[3,4,4,128]{2,3,1,0:T(8,128)S(1)} %copy-done, f32[3,4,4,128]{2,3,1,0:T(8,128)S(1)} %copy.42, f32[1,4,256,128]{2,3,1,0:T(8,128)S(1)} %bitcast.15, ...), kind=kLoop, calls=%fused_computation.90 | loop fusion | flops 861696 | bytes 2297856 | tf_op jit(solution)/shard_map/mul | solution.py:84
  51.9 1.3 %collective-permute-done.3 = f32[2,4,272,8]{2,3,1,0:T(8,128)S(1)} collective-permute-done((f32[2,4,272,8]{2,3,1,0:T(8,128)S(1)}, f32[2,4,272,8]{2,3,1,0:T(8,128)S(1)}, u32[]{:S(2)}, u32[]{:S(2)}) %collective-permute-start.3) | collective-permute-done | bytes 69664 | tf_op jit(solution)/shard_map/ppermute | solution.py:19
  53.8 1.8 %pad_maximum_fusion.1 = f32[2,4,272,144]{2,3,1,0:T(8,128)S(1)} fusion(f32[2,4,272,8]{2,3,1,0:T(8,128)S(1)} %collective-permute-done.3, f32[2,4,8,128]{2,3,1,0:T(8,128)} %collective-permute-done.1, f32[1,4,256,128]{2,3,1,0:T(8,128)S(1)} %copy.36, f32[1,4,256,128]{2,3,1,0:T(8,128)S(1)} %copy.35, f32[2,4,8,128]{2,3,1,0:T(8,128)} %collective-permute-done, ...), kind=kLoop, calls=%fused_computation.13 | loop fusion | flops 1566720 | bytes 2506752 | tf_op jit(solution)/shard_map/concatenate | solution.py:15
  56.6 10.9 %fusion.28 = f32[2,4,264,136]{2,3,1,0:T(8,128)S(1)} fusion(f32[1,4,264,136]{2,3,1,0:T(8,128)} %broadcast_multiply_fusion, f32[2,4,8,128]{2,3,1,0:T(8,128)} %collective-permute-done.1, f32[1,4,256,128]{2,3,1,0:T(8,128)S(1)} %copy.36, f32[1,4,256,128]{2,3,1,0:T(8,128)S(1)} %copy.35, f32[2,4,8,128]{2,3,1,0:T(8,128)} %collective-permute-done, ...), kind=kLoop, calls=%fused_computation.52 | loop fusion | flops 11776512 | bytes 22221312 | tf_op jit(solution)/shard_map/mul | solution.py:87
  68.7 4.3 %fusion.32 = f32[2,4,256,128]{2,3,1,0:T(8,128)S(1)} fusion(f32[1,4,256,128]{2,3,1,0:T(8,128)S(1)} %copy.36, f32[1,4,256,128]{2,3,1,0:T(8,128)S(1)} %copy.35, f32[2,4,256,128]{2,3,1,0:T(8,128)S(1)} %slice.317, f32[2,4,264,136]{2,3,1,0:T(8,128)S(1)} %fusion.28, f32[1,4,256,128]{2,3,1,0:T(8,128)S(1)} %copy-done.1, f32[4,256,128]{1,2,0:T(8,128)S(1)} %copy.37, ...), kind=kLoop, calls=%fused_computation.62 | loop fusion | flops 8912896 | bytes 21233664 | tf_op jit(solution)/shard_map/mul | solution.py:91
  73.6 34.8 %reshape.418 = f32[2,2,128,2,64,2]{5,4,3,2,1,0:T(8,128)} reshape(f32[1,4,256,128]{3,2,1,0:T(8,128)S(1)} %copy.48) | data formatting | bytes 1048576 | tf_op jit(solution)/shard_map/reshape | solution.py:97
  108.4 12.2 %reduce_sum.16 = f32[2,128,64]{2,1,0:T(8,128)S(1)} reduce(f32[2,2,128,2,64,2]{5,4,3,2,1,0:T(8,128)} %reshape.418, f32[]{:T(128)} %constant.23.clone.1), dimensions={1,3,5}, to_apply=%region_0.1 | reduce | flops 114688 | bytes 589828 | tf_op jit(solution)/shard_map/reduce_sum | solution.py:99
  120.7 1.9 %all-gather = f32[4,128,64]{1,2,0:T(8,128)S(1)} all-gather(f32[2,128,64]{1,2,0:T(8,128)S(1)} %broadcast_multiply_fusion.5), channel_id=2, replica_groups=mesh['shot'=2,'gy'=4,'gx'=4] {'shot'}, dimensions={0}, use_global_device_ids=true | all-gather | bytes 196608 | tf_op jit(solution)/shard_map/all_gather | solution.py:107
  122.7 0.7 broadcast_multiply_fusion.4
  (60 shorter events, 9.1 us)
Async XLA Ops:
  0.0 2.6 %copy-start.4 = (f32[1,4,256,128]{3,2,1,0:T(8,128)S(1)}, f32[1,4,256,128]{3,2,1,0:T(8,128)}, u32[]{:S(2)}) copy-start(f32[1,4,256,128]{3,2,1,0:T(8,128)} %param.11) | copy-start | bytes 1572868
  3.5 7.8 %copy-start.5 = (f32[1,4,256,128]{3,2,1,0:T(8,128)S(1)}, f32[1,4,256,128]{3,2,1,0:T(8,128)}, u32[]{:S(2)}) copy-start(f32[1,4,256,128]{3,2,1,0:T(8,128)} %param.12) | copy-start | bytes 1572868
  3.5 26.7 %collective-permute-start.4 = (f32[3,4,4,128]{3,2,1,0:T(4,128)S(1)}, f32[3,4,4,128]{3,2,1,0:T(4,128)S(1)}, u32[]{:S(2)}, u32[]{:S(2)}) collective-permute-start(f32[3,4,4,128]{3,2,1,0:T(4,128)S(1)} %copy.40), channel_id=1, source_target_pairs={{0,4},{4,8},{8,12},{1,5},{5,9},{9,13},{2,6},{6,10},{10,14},{3,7},{... | collective-permute-start | bytes 73736 | tf_op jit(solution)/shard_map/ppermute | solution.py:17
  8.8 21.8 %collective-permute-start.5 = (f32[3,4,4,128]{3,2,1,0:T(4,128)S(1)}, f32[3,4,4,128]{3,2,1,0:T(4,128)S(1)}, u32[]{:S(2)}, u32[]{:S(2)}) collective-permute-start(f32[3,4,4,128]{3,2,1,0:T(4,128)S(1)} %copy.41), channel_id=1, source_target_pairs={{4,0},{8,4},{12,8},{5,1},{9,5},{13,9},{6,2},{10,6},{14,10},{7,3},{... | collective-permute-start | bytes 73736 | tf_op jit(solution)/shard_map/ppermute | solution.py:19
  11.3 8.0 %copy-start.8 = (s32[1,3]{1,0:T(1,128)S(1)}, s32[1,3]{1,0:T(1,128)}, u32[]{:S(2)}) copy-start(s32[1,3]{1,0:T(1,128)} %param.16) | copy-start | bytes 40
  11.3 11.3 %copy-start.10 = (s32[1,4]{1,0:T(1,128)S(1)}, s32[1,4]{1,0:T(1,128)}, u32[]{:S(2)}) copy-start(s32[1,4]{1,0:T(1,128)} %param.15) | copy-start | bytes 52
  11.3 11.6 %copy-start.9 = (f32[1,2]{1,0:T(1,128)S(1)}, f32[1,2]{1,0:T(1,128)}, u32[]{:S(2)}) copy-start(f32[1,2]{1,0:T(1,128)} %param.14) | copy-start | bytes 28
  12.7 25.0 %collective-permute-start = (f32[2,4,8,128]{2,3,1,0:T(8,128)}, f32[2,4,8,128]{2,3,1,0:T(8,128)}, u32[]{:S(2)}, u32[]{:S(2)}) collective-permute-start(f32[2,4,8,128]{2,3,1,0:T(8,128)} %get-tuple-element.15), channel_id=1, source_target_pairs={{0,4},{4,8},{8,12},{1,5},{5,9},{9,13},{2,6},{6,10},{10,14},{3,7},{... | collective-permute-start | bytes 98312 | tf_op jit(solution)/shard_map/ppermute | solution.py:17
  18.0 24.2 %collective-permute-start.1 = (f32[2,4,8,128]{2,3,1,0:T(8,128)}, f32[2,4,8,128]{2,3,1,0:T(8,128)}, u32[]{:S(2)}, u32[]{:S(2)}) collective-permute-start(f32[2,4,8,128]{2,3,1,0:T(8,128)} %get-tuple-element.16), channel_id=1, source_target_pairs={{4,0},{8,4},{12,8},{5,1},{9,5},{13,9},{6,2},{10,6},{14,10},{7,3},{... | collective-permute-start | bytes 98312 | tf_op jit(solution)/shard_map/ppermute | solution.py:19
  32.7 15.5 %copy-start = (f32[3,4,4,128]{2,3,1,0:T(8,128)S(1)}, f32[3,4,4,128]{2,3,1,0:T(8,128)}, u32[]{:S(2)}) copy-start(f32[3,4,4,128]{2,3,1,0:T(8,128)} %copy.43) | copy-start | bytes 73732
  32.7 15.4 %collective-permute-start.6 = (f32[3,4,264,4]{2,3,1,0:T(4,128)S(1)}, f32[3,4,264,4]{2,3,1,0:T(4,128)S(1)}, u32[]{:S(2)}, u32[]{:S(2)}) collective-permute-start(f32[3,4,264,4]{2,3,1,0:T(4,128)S(1)} %get-tuple-element.9), channel_id=1, source_target_pairs={{0,1},{1,2},{2,3},{4,5},{5,6},{6,7},{8,9},{9,10},{10,11},{12,13},{... | collective-permute-start | bytes 152072 | tf_op jit(solution)/shard_map/ppermute | solution.py:17
  36.3 11.8 %collective-permute-start.7 = (f32[3,4,264,4]{2,3,1,0:T(4,128)S(1)}, f32[3,4,264,4]{2,3,1,0:T(4,128)S(1)}, u32[]{:S(2)}, u32[]{:S(2)}) collective-permute-start(f32[3,4,264,4]{2,3,1,0:T(4,128)S(1)} %get-tuple-element.10), channel_id=1, source_target_pairs={{1,0},{2,1},{3,2},{5,4},{6,5},{7,6},{9,8},{10,9},{11,10},{13,12},{... | collective-permute-start | bytes 152072 | tf_op jit(solution)/shard_map/ppermute | solution.py:19
  43.2 8.7 %collective-permute-start.2 = (f32[2,4,272,8]{2,3,1,0:T(8,128)S(1)}, f32[2,4,272,8]{2,3,1,0:T(8,128)S(1)}, u32[]{:S(2)}, u32[]{:S(2)}) collective-permute-start(f32[2,4,272,8]{2,3,1,0:T(8,128)S(1)} %get-tuple-element.12), channel_id=1, source_target_pairs={{0,1},{1,2},{2,3},{4,5},{5,6},{6,7},{8,9},{9,10},{10,11},{12,13},{... | collective-permute-start | bytes 208904 | tf_op jit(solution)/shard_map/ppermute | solution.py:17
  46.7 6.5 %collective-permute-start.3 = (f32[2,4,272,8]{2,3,1,0:T(8,128)S(1)}, f32[2,4,272,8]{2,3,1,0:T(8,128)S(1)}, u32[]{:S(2)}, u32[]{:S(2)}) collective-permute-start(f32[2,4,272,8]{2,3,1,0:T(8,128)S(1)} %get-tuple-element.11), channel_id=1, source_target_pairs={{1,0},{2,1},{3,2},{5,4},{6,5},{7,6},{9,8},{10,9},{11,10},{13,12},{... | collective-permute-start | bytes 208904 | tf_op jit(solution)/shard_map/ppermute | solution.py:19
  53.2 0.6 copy-start.6
  55.6 1.0 copy-start.2
  55.6 1.0 copy-start.7
  67.5 1.0 copy-start.1
  67.6 1.1 copy-start.3
